TPU v7x, 32 devices: a whole 2x2x4 slice. The times are simulated.
32 devices in a mesh: leaf: 8 (over z, x), row: 2 (over y), col: 2 (over core).
Axes of the slice: x: 2, y: 2, z: 4, core: 2. Of those that a mesh axis runs over, the one named last changes fastest.
Arguments:
- leaf_rhs: bfloat16 [8, 4096, 128], P('leaf', ('row', 'col')), may hold values from -6 to 6
- leaf_factor: bfloat16 [8, 4096, 4096], P('leaf', ('row', 'col')), as said below
- leaf_coupling: bfloat16 [8, 4096, 4096], P('leaf', None, ('row', 'col')), may hold values from -0.046875 to 0.046875
- border_rows: int32 [8, 4096], P('leaf'), may hold values from 0 to 4095, as said below
- border_count: int32 [8], P('leaf'), may hold values from 1024 to 4096, as said below
- separator_rhs: bfloat16 [4096, 128], P(('leaf', 'row', 'col')), may hold values from -6 to 6
- separator_factor: bfloat16 [4096, 4096], P(('leaf', 'row', 'col')), as said below
Outputs:
- leaf_solution: float32 [8, 4096, 128], P('leaf', ('row', 'col'))
- separator_solution: float32 [4096, 128], P(('leaf', 'row', 'col'))
Inputs may be any that keep to these rules, and one draw needn't show every extreme that they name: `border_rows`: the 4096 row numbers of one section are distinct. Border rows j < border_count[k] of section k are live, the others are unused; some section has all 4096 live. `leaf_factor`: lower triangular with a positive diagonal. `separator_factor`: lower triangular with a positive diagonal.
All inputs are finite; a program needn't handle non-finite values.
Results may differ from a plain program's by a relative error of at most 0.013.
Values may be sent and summed in bfloat16 or wider, within the bound.
No kernel may reach another device: no remote copies, remote signals or barrier semaphores. Data moves between devices by JAX's collectives and lax.ppermute only.
A program may use at most 64 MiB of HBM per device.

v0:
```python
import jax
import jax.numpy as jnp
from jax import lax
from jax.sharding import PartitionSpec as P


def local(
    leaf_rhs, leaf_factor, leaf_coupling, border_rows, border_count, separator_rhs, separator_factor
):
    contract_first = (((0,), (0,)), ((), ()))
    rhs_local = leaf_rhs[0]
    factor_local = leaf_factor[0]
    coupling = leaf_coupling[0]
    index_set = border_rows[0]
    live = jnp.arange(index_set.shape[0], dtype=jnp.int32) < border_count[0]
    columns = rhs_local.shape[1]
    block = factor_local
    forward = jnp.dot(
        block,
        lax.all_gather(rhs_local, ("row", "col"), axis=0, tiled=True),
        preferred_element_type=jnp.float32,
    ).astype(jnp.bfloat16)
    update = jnp.dot(coupling, forward, preferred_element_type=jnp.float32)
    update = jnp.where(live[:, None], update, 0.0)
    sep_rows = separator_factor.shape[0]
    sep_order = separator_factor.shape[1]
    position = lax.axis_index(("leaf", "row", "col")) * sep_rows
    placed = lax.dynamic_update_slice_in_dim(
        jnp.zeros((sep_order, columns), jnp.float32), separator_rhs.astype(jnp.float32), position, 0
    )
    placed = placed.at[index_set].add(-update)
    whole = lax.psum(placed, ("leaf", "row", "col")).astype(jnp.bfloat16)
    root_forward = jnp.dot(separator_factor, whole, preferred_element_type=jnp.float32).astype(
        jnp.bfloat16
    )
    partial_terms = lax.dot_general(
        separator_factor, root_forward, contract_first, preferred_element_type=jnp.float32
    )
    totals = lax.psum(partial_terms, ("leaf", "row", "col"))
    separator_solution = lax.dynamic_slice_in_dim(totals, position, sep_rows, 0)
    rounded = totals.astype(jnp.bfloat16)
    border = jnp.where(live[:, None], rounded[index_set], jnp.zeros((), jnp.bfloat16))
    corrected = (
        forward.astype(jnp.float32)
        - lax.dot_general(coupling, border, contract_first, preferred_element_type=jnp.float32)
    ).astype(jnp.bfloat16)
    block = factor_local
    solution = lax.psum_scatter(
        lax.dot_general(
            block, corrected, contract_first, preferred_element_type=jnp.float32
        ).astype(jnp.bfloat16),
        ("row", "col"),
        scatter_dimension=0,
        tiled=True,
    ).astype(jnp.float32)
    return (solution[None], separator_solution)


def solution(mesh):
    placed = (
        P("leaf", ("row", "col"), None),
        P("leaf", ("row", "col"), None),
        P("leaf", None, ("row", "col")),
        P("leaf", None),
        P("leaf"),
        P(("leaf", "row", "col"), None),
        P(("leaf", "row", "col"), None),
    )
    return jax.shard_map(
        local,
        mesh=mesh,
        in_specs=placed,
        out_specs=(P("leaf", ("row", "col"), None), P(("leaf", "row", "col"), None)),
        check_vma=False,
    )
```

profile of v0, /device:TPU:0, one launch (start us, length us, event | category | flops | bytes accessed | tf_op | source)
XLA Modules:
  0.0 322.0 jit_solution(7589405319605890312)
XLA Ops:
  7.2 0.0 copy-start
  7.2 0.0 copy-start.2
  7.2 0.0 copy-start.3
  7.2 0.0 all-gather.3.cloned.1.call-start
  7.2 0.7 all-gather.3.cloned.1.call-update
  7.9 0.0 all-reduce.3.cloned.1.call-start
  8.6 0.1 broadcast_in_dim.38
  8.8 0.0 copy-done.2
  8.8 0.0 copy-done.3
  8.9 20.2 %all-gather.3.cloned.1.call-done = bf16[1,4096,128]{2,1,0:T(8,128)(2,1)} async-done(((bf16[1,1024,128]{2,1,0:T(8,128)(2,1)}), bf16[1,4096,128]{2,1,0:T(8,128)(2,1)}) %all-gather.3.cloned.1.call-update) | async-done | bytes 1048592 | tf_op jit(solution)/shard_map/all_gather | solution.py:20
  29.0 0.0 copy-start.1
  29.0 6.1 %fusion.32 = bf16[1024,128]{1,0:T(8,128)(2,1)S(1)} fusion(bf16[1,1024,4096]{2,1,0:T(8,128)(2,1)} %param.8, bf16[1,4096,128]{2,1,0:T(8,128)(2,1)} %all-gather.3.cloned.1.call-done), kind=kOutput, calls=%fused_computation.19 | convolution fusion | flops 1073872896 | bytes 9699328 | tf_op jit(solution)/shard_map/dot_general | solution.py:18
  35.1 0.0 copy-done.1
  35.1 4.4 %fusion.17 = f32[4096,128]{1,0:T(8,128)} fusion(bf16[1024,128]{1,0:T(8,128)(2,1)S(1)} %fusion.32, bf16[1,4096,1024]{2,1,0:T(8,128)(2,1)S(1)} %copy-done.1, pred[4096]{0:T(1024)(128)(4,1)S(1)} %iota_compare_fusion), kind=kOutput, calls=%fused_computation.14 | convolution fusion | flops 1074790400 | bytes 10752000 | tf_op jit(solution)/shard_map/dot_general | solution.py:23
  39.5 23.4 %scatter_fusion = f32[4096,128]{1,0:T(8,128)S(1)} fusion(f32[4096,128]{1,0:T(8,128)S(1)} %convert_dynamic-update-slice_fusion, s32[4096]{0:T(1024)S(1)} %bitcast.59, f32[4096,128]{1,0:T(8,128)} %fusion.17), kind=kCustom, calls=%fused_computation.1 | custom fusion | flops 524288 | bytes 6307840 | tf_op jit(solution)/shard_map/scatter-add | solution.py:31
  63.0 62.4 %all-reduce.4 = bf16[4096,128]{1,0:T(8,128)(2,1)} all-reduce(f32[4096,128]{1,0:T(8,128)S(1)} %scatter_fusion), channel_id=1, replica_groups=mesh['leaf'=8,'row'=2,'col'=2] {'leaf','row','col'}, use_global_device_ids=true, to_apply=%region_1.2 | all-reduce | flops 524288 | bytes 3145728 | tf_op jit(solution)/shard_map/psum | solution.py:32
  125.3 0.0 copy-done
  125.3 3.9 %convolution_bitcast_fusion = f32[4096,128]{0,1:T(8,128)} fusion(bf16[128,4096]{1,0:T(8,128)(2,1)S(1)} %copy-done, bf16[4096,128]{1,0:T(8,128)(2,1)} %all-reduce.4), kind=kOutput, calls=%fused_computation.10 | convolution fusion | flops 268451840 | bytes 4194304 | tf_op jit(solution)/shard_map/dot_general | solution.py:36
  129.2 0.0 all-reduce.3.cloned.1.call-update
  129.2 0.2 reduce-scatter.2.cloned.1.call-start
  129.5 133.4 %all-reduce.3.cloned.1.call-done = f32[4096,128]{0,1:T(8,128)} async-done(((f32[4096,128]{0,1:T(8,128)}), f32[4096,128]{0,1:T(8,128)}) %all-reduce.3.cloned.1.call-update) | async-done | bytes 2097168 | tf_op jit(solution)/shard_map/psum | solution.py:39
  262.8 1.7 convert_element_type.34
  264.6 0.7 copy.12
  265.2 12.1 %gather_fusion = bf16[4096,128]{1,0:T(8,128)(2,1)S(1)} fusion(bf16[4096,128]{1,0:T(8,128)(2,1)S(1)} %copy.12, s32[4096]{0:T(1024)S(1)} %broadcast_clamp_fusion), kind=kCustom, calls=%fused_computation | custom fusion | bytes 2113536 | tf_op jit(solution)/shard_map/gather | solution.py:42
  277.4 12.4 %fusion.20 = bf16[4096,128]{0,1:T(8,128)(2,1)} fusion(bf16[1,1024,4096]{2,1,0:T(8,128)(2,1)} %param.8, bf16[1,4096,1024]{2,1,0:T(8,128)(2,1)} %param.9, bf16[4096,128]{1,0:T(8,128)(2,1)S(1)} %gather_fusion, pred[4096]{0:T(1024)(128)(4,1)S(1)} %iota_compare_fusion, bf16[1024,128]{1,0:T(8,128)(2,1)S(1)} %fusion.32), kind=kOutput, calls=%fused_computation.15 | convolution fusion | flops 2148925440 | bytes 19140608 | tf_op jit(solution)/shard_map/dot_general | solution.py:49
  289.8 0.0 reduce-scatter.2.cloned.1.call-update
  289.8 0.9 constant_dynamic-slice_fusion
  290.6 0.7 copy.14
  291.4 22.1 %reduce-scatter.2.cloned.1.call-done = bf16[1024,128]{0,1:T(8,128)(2,1)} async-done(((bf16[4096,128]{0,1:T(8,128)(2,1)}), bf16[1024,128]{0,1:T(8,128)(2,1)}) %reduce-scatter.2.cloned.1.call-update) | async-done | bytes 262160 | tf_op jit(solution)/shard_map/reduce_scatter | solution.py:48
  313.5 1.0 bitcast_convert_fusion
  314.5 1.0 copy.13
  (4 shorter events, 0.0 us)
Async XLA Ops:
  7.2 118.2 %copy-start = (bf16[128,4096]{1,0:T(8,128)(2,1)S(1)}, bf16[128,4096]{1,0:T(8,128)(2,1)}, u32[]{:S(2)}) copy-start(bf16[128,4096]{1,0:T(8,128)(2,1)} %param.13) | copy-start | bytes 3145732
  7.2 1.6 copy-start.2
  7.2 1.6 copy-start.3
  7.2 21.8 %all-gather.3.cloned.1.call-start = ((), (), s32[]{:S(2)}) async-start(), calls=%async_computation.3 | async-start | bytes 1310720 | tf_op jit(solution)/shard_map/all_gather | solution.py:20
  7.9 254.9 %all-reduce.3.cloned.1.call-start = ((), (), s32[]{:S(2)}) async-start(), calls=%async_computation.1 | async-start | bytes 4194304 | tf_op jit(solution)/shard_map/psum | solution.py:39
  29.0 6.1 %copy-start.1 = (bf16[1,4096,1024]{2,1,0:T(8,128)(2,1)S(1)}, bf16[1,4096,1024]{2,1,0:T(8,128)(2,1)}, u32[]{:S(2)}) copy-start(bf16[1,4096,1024]{2,1,0:T(8,128)(2,1)} %param.9) | copy-start | bytes 25165828
  129.2 184.3 %reduce-scatter.2.cloned.1.call-start = ((), (), s32[]{:S(2)}) async-start(), calls=%async_computation.2 | async-start | bytes 1310720 | tf_op jit(solution)/shard_map/reduce_scatter | solution.py:48
Sparse Core Ops, SparseCore 0:
  9.6 19.4 all-gather.2
  129.4 133.4 all-reduce.2
  289.9 23.5 reduce-scatter.1
where the time goes:
time: 322 us
  waiting for transfers between devices  176 us (55%)
  blocking collectives  62.4 us (19%)
  matrix products  26.7 us (8%)
  other arithmetic  26.2 us (8%)
  local copies, waits for them, and re-layouts  15.5 us (5%)
  between operations  14.5 us (5%)
    psum x1, waiting for transfers between devices, local(): totals = lax.psum(partial_terms, ('leaf', 'row', 'col'))  133 us
    psum x1, blocking collectives, local(): whole = lax.psum(placed, ('leaf', 'row', 'col')).astype(jnp.bfloat16)  62.4 us
    scatter-add x1, other arithmetic, local(): placed = placed.at[index_set].add(-update)  23.4 us
    reduce_scatter x1, waiting for transfers between devices, local(): lax.psum_scatter(lax.dot_general(block, corrected, contract_first, prefer...  22.1 us
    all_gather x1, waiting for transfers between devices, local(): lax.all_gather(rhs_local, ('row', 'col'), axis=0, tiled=True)  20.2 us
    dot_general x1, matrix products, local(): lax.dot_general(block, corrected, contract_first, preferred_element_type=...  12.4 us
    gather x1, local copies, waits for them, and re-layouts, local(): rounded[index_set]  12.1 us
  transfers between devices with their start and end apart: 3, of which 3 were waited for; matrix products, arithmetic and copies ran while one was open for 1% of the time, Pallas kernels for 0%

commit v1 on v0

--- a/solution.py
+++ b/solution.py
@@ -29,7 +29,7 @@
         jnp.zeros((sep_order, columns), jnp.float32), separator_rhs.astype(jnp.float32), position, 0
     )
     placed = placed.at[index_set].add(-update)
-    whole = lax.psum(placed, ("leaf", "row", "col")).astype(jnp.bfloat16)
+    whole = lax.psum(lax.psum(placed, "leaf"), ("row", "col")).astype(jnp.bfloat16)
     root_forward = jnp.dot(separator_factor, whole, preferred_element_type=jnp.float32).astype(
         jnp.bfloat16
     )

time: 322 us -> 404 us (1.25)
  waiting for transfers between devices: 176 us -> 280 us
  blocking collectives: 62.4 us -> 41 us
    psum x0 -> x1, waiting for transfers between devices: none -> 102 us  [local(): lax.psum(placed, 'leaf')]
    psum x1, blocking collectives: 62.4 us -> 41 us  [local(): lax.psum(lax.psum(placed, 'leaf'), ('row', 'col')).astype(jnp.bfloat16)]
  transfers between devices with their start and end apart: 3 -> 4, of which waited for: 3 -> 4; matrix products, arithmetic and copies ran while one was open for 1% -> 0% of each run, Pallas kernels for 0% -> 0%
where the time goes in v1:
time: 404 us
  waiting for transfers between devices  280 us (69%)
  blocking collectives  41 us (10%)
  other arithmetic  26.2 us (6%)
  matrix products  25.5 us (6%)
  local copies, waits for them, and re-layouts  16.8 us (4%)
  between operations  14.6 us (4%)
    psum x1, waiting for transfers between devices, local(): totals = lax.psum(partial_terms, ('leaf', 'row', 'col'))  134 us
    psum x1, waiting for transfers between devices, local(): lax.psum(placed, 'leaf')  102 us
    psum x1, blocking collectives, local(): lax.psum(lax.psum(placed, 'leaf'), ('row', 'col')).astype(jnp.bfloat16)  41 us
    scatter-add x1, other arithmetic, local(): placed = placed.at[index_set].add(-update)  23.4 us
    reduce_scatter x1, waiting for transfers between devices, local(): lax.psum_scatter(lax.dot_general(block, corrected, contract_first, prefer...  22.1 us
    all_gather x1, waiting for transfers between devices, local(): lax.all_gather(rhs_local, ('row', 'col'), axis=0, tiled=True)  20.2 us
    dot_general x1, matrix products, local(): lax.dot_general(block, corrected, contract_first, preferred_element_type=...  12.4 us
    gather x1, local copies, waits for them, and re-layouts, local(): rounded[index_set]  12.1 us
  transfers between devices with their start and end apart: 4, of which 4 were waited for; matrix products, arithmetic and copies ran while one was open for 0% of the time, Pallas kernels for 0%

profile of v1, /device:TPU:0, one launch (start us, length us, event | category | flops | bytes accessed | tf_op | source)
XLA Modules:
  0.0 404.0 jit_solution(13632580934254791846)
XLA Ops:
  7.2 0.0 copy-start
  7.2 0.0 copy-start.3
  7.2 0.0 copy-start.4
  7.2 0.0 all-gather.3.cloned.1.call-start
  7.2 0.7 all-gather.3.cloned.1.call-update
  7.9 0.0 all-reduce.4.cloned.1.call-start
  8.6 0.1 broadcast_in_dim.38
  8.8 0.0 copy-done.3
  8.8 0.0 copy-done.4
  8.9 20.2 %all-gather.3.cloned.1.call-done = bf16[1,4096,128]{2,1,0:T(8,128)(2,1)} async-done(((bf16[1,1024,128]{2,1,0:T(8,128)(2,1)}), bf16[1,4096,128]{2,1,0:T(8,128)(2,1)}) %all-gather.3.cloned.1.call-update) | async-done | bytes 1048592 | tf_op jit(solution)/shard_map/all_gather | solution.py:20
  29.0 0.0 copy-start.2
  29.0 6.1 %fusion.32 = bf16[1024,128]{1,0:T(8,128)(2,1)S(1)} fusion(bf16[1,1024,4096]{2,1,0:T(8,128)(2,1)} %param.8, bf16[1,4096,128]{2,1,0:T(8,128)(2,1)} %all-gather.3.cloned.1.call-done), kind=kOutput, calls=%fused_computation.19 | convolution fusion | flops 1073872896 | bytes 9699328 | tf_op jit(solution)/shard_map/dot_general | solution.py:18
  35.1 0.0 copy-done.2
  35.1 4.4 %fusion.17 = f32[4096,128]{1,0:T(8,128)} fusion(bf16[1024,128]{1,0:T(8,128)(2,1)S(1)} %fusion.32, bf16[1,4096,1024]{2,1,0:T(8,128)(2,1)S(1)} %copy-done.2, pred[4096]{0:T(1024)(128)(4,1)S(1)} %iota_compare_fusion), kind=kOutput, calls=%fused_computation.14 | convolution fusion | flops 1074790400 | bytes 10752000 | tf_op jit(solution)/shard_map/dot_general | solution.py:23
  39.5 23.4 %scatter_fusion = f32[4096,128]{1,0:T(8,128)S(1)} fusion(f32[4096,128]{1,0:T(8,128)S(1)} %convert_dynamic-update-slice_fusion, s32[4096]{0:T(1024)S(1)} %bitcast.59, f32[4096,128]{1,0:T(8,128)} %fusion.17), kind=kCustom, calls=%fused_computation.1 | custom fusion | flops 524288 | bytes 6307840 | tf_op jit(solution)/shard_map/scatter-add | solution.py:31
  63.0 0.0 copy-start.1
  63.0 1.3 copy-done.1
  64.3 0.0 all-reduce.4.cloned.1.call-update
  64.3 0.0 all-reduce.6.cloned.1.call-start
  64.4 102.4 %all-reduce.4.cloned.1.call-done = f32[4096,128]{1,0:T(8,128)} async-done(((f32[4096,128]{1,0:T(8,128)}), f32[4096,128]{1,0:T(8,128)}) %all-reduce.4.cloned.1.call-update) | async-done | bytes 2097168 | tf_op jit(solution)/shard_map/psum | solution.py:32
  166.8 41.0 %all-reduce.7 = bf16[4096,128]{1,0:T(8,128)(2,1)S(1)} all-reduce(f32[4096,128]{1,0:T(8,128)} %all-reduce.4.cloned.1.call-done), channel_id=1, replica_groups=mesh['leaf'=8,'row'=2,'col'=2] {'row','col'}, use_global_device_ids=true, to_apply=%region_2.3 | all-reduce | flops 524288 | bytes 3145728 | tf_op jit(solution)/shard_map/psum | solution.py:32
  207.7 0.0 copy-done
  207.8 2.6 convolution_bitcast_fusion
  210.4 0.0 all-reduce.6.cloned.1.call-update
  210.4 0.2 reduce-scatter.2.cloned.1.call-start
  210.7 134.2 %all-reduce.6.cloned.1.call-done = f32[4096,128]{0,1:T(8,128)} async-done(((f32[4096,128]{0,1:T(8,128)}), f32[4096,128]{0,1:T(8,128)}) %all-reduce.6.cloned.1.call-update) | async-done | bytes 2097168 | tf_op jit(solution)/shard_map/psum | solution.py:39
  344.8 1.7 convert_element_type.34
  346.6 0.7 copy.12
  347.2 12.1 %gather_fusion = bf16[4096,128]{1,0:T(8,128)(2,1)S(1)} fusion(bf16[4096,128]{1,0:T(8,128)(2,1)S(1)} %copy.12, s32[4096]{0:T(1024)S(1)} %broadcast_clamp_fusion), kind=kCustom, calls=%fused_computation | custom fusion | bytes 2113536 | tf_op jit(solution)/shard_map/gather | solution.py:42
  359.4 12.4 %fusion.20 = bf16[4096,128]{0,1:T(8,128)(2,1)} fusion(bf16[1,1024,4096]{2,1,0:T(8,128)(2,1)} %param.8, bf16[1,4096,1024]{2,1,0:T(8,128)(2,1)} %param.9, bf16[4096,128]{1,0:T(8,128)(2,1)S(1)} %gather_fusion, pred[4096]{0:T(1024)(128)(4,1)S(1)} %iota_compare_fusion, bf16[1024,128]{1,0:T(8,128)(2,1)S(1)} %fusion.32), kind=kOutput, calls=%fused_computation.15 | convolution fusion | flops 2148925440 | bytes 19140608 | tf_op jit(solution)/shard_map/dot_general | solution.py:49
  371.8 0.0 reduce-scatter.2.cloned.1.call-update
  371.8 0.9 constant_dynamic-slice_fusion
  372.7 0.7 copy.14
  373.4 22.1 %reduce-scatter.2.cloned.1.call-done = bf16[1024,128]{0,1:T(8,128)(2,1)} async-done(((bf16[4096,128]{0,1:T(8,128)(2,1)}), bf16[1024,128]{0,1:T(8,128)(2,1)}) %reduce-scatter.2.cloned.1.call-update) | async-done | bytes 262160 | tf_op jit(solution)/shard_map/reduce_scatter | solution.py:48
  395.5 1.0 bitcast_convert_fusion
  396.5 1.0 copy.13
  (4 shorter events, 0.0 us)
Async XLA Ops:
  7.2 200.6 %copy-start = (bf16[128,4096]{1,0:T(8,128)(2,1)S(1)}, bf16[128,4096]{1,0:T(8,128)(2,1)}, u32[]{:S(2)}) copy-start(bf16[128,4096]{1,0:T(8,128)(2,1)} %param.13) | copy-start | bytes 3145732
  7.2 1.6 copy-start.3
  7.2 1.6 copy-start.4
  7.2 21.8 %all-gather.3.cloned.1.call-start = ((), (), s32[]{:S(2)}) async-start(), calls=%async_computation.4 | async-start | bytes 1310720 | tf_op jit(solution)/shard_map/all_gather | solution.py:20
  7.9 158.8 %all-reduce.4.cloned.1.call-start = ((), (), s32[]{:S(2)}) async-start(), calls=%async_computation.1 | async-start | bytes 4194304 | tf_op jit(solution)/shard_map/psum | solution.py:32
  29.0 6.1 %copy-start.2 = (bf16[1,4096,1024]{2,1,0:T(8,128)(2,1)S(1)}, bf16[1,4096,1024]{2,1,0:T(8,128)(2,1)}, u32[]{:S(2)}) copy-start(bf16[1,4096,1024]{2,1,0:T(8,128)(2,1)} %param.9) | copy-start | bytes 25165828
  63.0 1.3 copy-start.1
  64.3 280.5 %all-reduce.6.cloned.1.call-start = ((), (), s32[]{:S(2)}) async-start(), calls=%async_computation.2 | async-start | bytes 4194304 | tf_op jit(solution)/shard_map/psum | solution.py:39
  210.4 185.1 %reduce-scatter.2.cloned.1.call-start = ((), (), s32[]{:S(2)}) async-start(), calls=%async_computation.3 | async-start | bytes 1310720 | tf_op jit(solution)/shard_map/reduce_scatter | solution.py:48
Sparse Core Ops, SparseCore 0:
  9.6 19.4 all-gather.2
  64.4 102.2 all-reduce.3
  210.5 134.2 all-reduce.5
  371.9 23.5 reduce-scatter.1
